TPU v7x, 32 devices: a whole 2x2x4 slice. The times are simulated.
32 devices in a mesh: fsdp: 4 (over y, core), ctx: 2 (over x), tp: 4 (over z).
Axes of the slice: x: 2, y: 2, z: 4, core: 2. Of those that a mesh axis runs over, the one named last changes fastest.
Arguments:
- inputs: bfloat16 [2, 8, 512, 1024], P(None, 'fsdp', 'ctx'), may hold values from -6 to 6
- out_grad: bfloat16 [2, 8, 512, 1024], P(None, 'fsdp', 'ctx'), may hold values from -6 to 6
- segment_ids: int32 [2, 8, 512], P(None, 'fsdp'), may hold values from 0 to 7, never falling along the last dimension, each value on 1 to 256 neighbouring positions
- w_qkv: bfloat16 [1024, 3072], P(('fsdp', 'ctx'), 'tp'), may hold values from -0.25 to 0.25
- bias_qv: bfloat16 [2048], P('tp'), may hold values from -3 to 3
- w_out: bfloat16 [1024, 1024], P(('fsdp', 'ctx'), 'tp'), may hold values from -0.25 to 0.25
- w_up: bfloat16 [1024, 4096], P(('fsdp', 'ctx'), 'tp'), may hold values from -0.1875 to 0.1875
- bias_up: bfloat16 [4096], P('tp'), may hold values from -2 to 2
- w_down: bfloat16 [1024, 4096], P(('fsdp', 'ctx'), 'tp'), may hold values from -0.125 to 0.125
- gains: bfloat16 [1024, 2], P(('fsdp', 'ctx')), may hold values from 0.25 to 1.75
- shifts: bfloat16 [1024, 4], P(('fsdp', 'ctx')), may hold values from -2 to 2
Outputs:
- layer_out: bfloat16 [2, 8, 512, 1024], P(None, 'fsdp', ('ctx', 'tp'))
- input_grad: float32 [2, 8, 512, 1024], P(None, 'fsdp', ('ctx', 'tp'))
- grad_w_qkv: float32 [1024, 3072], P(('fsdp', 'ctx'), 'tp')
- grad_bias_qv: float32 [2048], P('tp')
- grad_w_out: float32 [1024, 1024], P(('fsdp', 'ctx'), 'tp')
- grad_w_up: float32 [1024, 4096], P(('fsdp', 'ctx'), 'tp')
- grad_bias_up: float32 [4096], P('tp')
- grad_w_down: float32 [1024, 4096], P(('fsdp', 'ctx'), 'tp')
- grad_gains: float32 [1024, 2], P(('fsdp', 'ctx'))
- grad_shifts: float32 [1024, 4], P(('fsdp', 'ctx'))
Inputs may be any that keep to these rules, and one draw needn't show every extreme that they name: `segment_ids`: within a sequence the ids never fall; each of the 8 documents holds 1 to 256 positions, and one holds exactly 256.
All inputs are finite; a program needn't handle non-finite values.
Results may differ from a plain program's by a relative error of at most 0.018.
Values may be sent and summed in bfloat16 or wider, within the bound.
A program may use at most 64 MiB of HBM per device.

v0:
```python
import jax
import jax.numpy as jnp
from jax import lax
from jax.sharding import PartitionSpec as P

HD = 64
norm_epsilon = 1e-12
masked_score = -1e30


def norm_rows(rows_in, gain_row, offset):
    average = jnp.mean(rows_in, axis=-1, keepdims=True)
    centered = rows_in - average
    spread = jnp.mean(centered * centered, axis=-1, keepdims=True)
    return centered * lax.rsqrt(spread + norm_epsilon) * gain_row + offset


def exact_gelu(rows_in):
    return jax.nn.gelu(rows_in, approximate=False)


def contract_rows(left_rows, right_rows):
    return lax.dot_general(
        left_rows, right_rows, (((0,), (0,)), ((), ())), preferred_element_type=jnp.float32
    )


def times_transposed(left_rows, right_rows):
    return lax.dot_general(
        left_rows, right_rows, (((1,), (1,)), ((), ())), preferred_element_type=jnp.float32
    )


def masked_scores(queries, key_rows, same_segment, score_scale):
    scores = (
        jnp.einsum("sqhe,skhe->shqk", queries, key_rows, preferred_element_type=jnp.float32)
        * score_scale
    )
    return jnp.where(same_segment[:, None], scores, masked_score)


def add_pair(running, update):
    return running + update


def reduce_rows(part):
    return lax.psum(part, "tp")


def local(
    inputs, out_grad, segment_ids, w_qkv, bias_qv, w_out, w_up, bias_up, w_down, gains, shifts
):
    batches, seq_local, rows_local, model_width = inputs.shape
    tokens = seq_local * rows_local
    heads_local = w_out.shape[1] // HD
    score_scale = HD ** (-0.5)
    row_share = rows_local // lax.axis_size("tp")
    row_start = lax.axis_index("tp") * row_share
    query_start = lax.axis_index("ctx") * rows_local
    qv_bias = bias_qv.astype(jnp.float32).reshape(heads_local, 2, HD)
    up_bias = bias_up.astype(jnp.float32)

    def pick_rows(values):
        shaped = values.reshape(seq_local, rows_local, model_width)
        return lax.dynamic_slice_in_dim(shaped, row_start, row_share, 1)

    full_totals = (
        jnp.zeros((model_width, w_qkv.shape[1]), jnp.float32),
        jnp.zeros((model_width, w_out.shape[1]), jnp.float32),
        jnp.zeros((model_width, w_up.shape[1]), jnp.float32),
        jnp.zeros((model_width, w_down.shape[1]), jnp.float32),
        jnp.zeros((model_width, 2), jnp.float32),
        jnp.zeros((model_width, 4), jnp.float32),
    )
    share_totals = (
        jnp.zeros(w_qkv.shape, jnp.float32),
        jnp.zeros(w_out.shape, jnp.float32),
        jnp.zeros(w_up.shape, jnp.float32),
        jnp.zeros(w_down.shape, jnp.float32),
        jnp.zeros(gains.shape, jnp.float32),
        jnp.zeros(shifts.shape, jnp.float32),
    )
    qv_bias_grad = jnp.zeros(bias_qv.shape, jnp.float32)
    up_bias_grad = jnp.zeros(bias_up.shape, jnp.float32)
    layer_rows = []
    input_rows = []
    for batch_index in range(batches):
        gathered = (
            lax.all_gather(w_qkv, ("fsdp", "ctx"), axis=0, tiled=True),
            lax.all_gather(w_out, ("fsdp", "ctx"), axis=0, tiled=True),
            lax.all_gather(w_up, ("fsdp", "ctx"), axis=0, tiled=True),
            lax.all_gather(w_down, ("fsdp", "ctx"), axis=0, tiled=True),
            lax.all_gather(gains, ("fsdp", "ctx"), axis=0, tiled=True),
            lax.all_gather(shifts, ("fsdp", "ctx"), axis=0, tiled=True),
        )
        full_qkv, full_out, full_up, full_down, full_gains, full_shifts = gathered
        gain_rows = full_gains.astype(jnp.float32)
        shift_rows = full_shifts.astype(jnp.float32)
        x_low = inputs[batch_index].reshape(tokens, model_width)
        x_full = x_low.astype(jnp.float32)
        projected = jnp.dot(x_low, full_qkv, preferred_element_type=jnp.float32)
        projected = projected.reshape(seq_local, rows_local, heads_local, 3, HD)
        queries = (projected[:, :, :, 0] + qv_bias[:, 0]).astype(jnp.bfloat16)
        key_local = projected[:, :, :, 1].astype(jnp.bfloat16)
        value_local = (projected[:, :, :, 2] + qv_bias[:, 1]).astype(jnp.bfloat16)
        joined = jnp.concatenate([key_local, value_local], axis=-1)
        joined_all = lax.all_gather(joined, "ctx", axis=1, tiled=True)
        key_rows = joined_all[..., :HD]
        value_rows = joined_all[..., HD:]
        segments = segment_ids[batch_index]
        query_segments = lax.dynamic_slice_in_dim(segments, query_start, rows_local, 1)
        same_segment = query_segments[:, :, None] == segments[:, None, :]
        scores = masked_scores(queries, key_rows, same_segment, score_scale)
        row_max = jnp.max(scores, axis=-1, keepdims=True)
        weights = jnp.exp(scores - row_max)
        row_total = jnp.sum(weights, axis=-1, keepdims=True)
        log_total = row_max + jnp.log(row_total)
        p_low = (weights / row_total).astype(jnp.bfloat16)
        attended = jnp.einsum(
            "shqk,skhe->sqhe", p_low, value_rows, preferred_element_type=jnp.float32
        )
        attended_low = attended.reshape(tokens, heads_local * HD).astype(jnp.bfloat16)
        attention_part = times_transposed(attended_low, full_out)
        upstream_full = out_grad[batch_index].reshape(tokens, model_width).astype(jnp.float32)
        attention_total = reduce_rows(attention_part)
        first_sum = x_full + attention_total + shift_rows[:, 0]
        first_norm, first_back = jax.vjp(norm_rows, first_sum, gain_rows[:, 0], shift_rows[:, 1])
        norm_low = first_norm.astype(jnp.bfloat16)
        before_act = jnp.dot(norm_low, full_up, preferred_element_type=jnp.float32) + up_bias
        activated, gelu_back = jax.vjp(exact_gelu, before_act)
        hidden = activated.astype(jnp.bfloat16)
        down_part = times_transposed(hidden, full_down)
        down_total = reduce_rows(down_part)
        second_sum = first_norm + down_total + shift_rows[:, 2]
        result, second_back = jax.vjp(norm_rows, second_sum, gain_rows[:, 1], shift_rows[:, 3])
        layer_rows.append(pick_rows(result).astype(jnp.bfloat16))
        second_grad, gain_two, shift_three = second_back(upstream_full)
        shift_two = jnp.sum(second_grad, axis=0)
        second_low = second_grad.astype(jnp.bfloat16)
        down_step = contract_rows(second_low, hidden)
        hidden_grad = jnp.dot(second_low, full_down, preferred_element_type=jnp.float32)
        (act_grad,) = gelu_back(hidden_grad)
        up_bias_grad = up_bias_grad + jnp.sum(act_grad, axis=0)
        act_low = act_grad.astype(jnp.bfloat16)
        up_step = contract_rows(norm_low, act_low)
        back_part = times_transposed(act_low, full_up)
        back_total = reduce_rows(back_part)
        norm_grad = second_grad + back_total
        first_grad, gain_one, shift_one = first_back(norm_grad)
        shift_zero = jnp.sum(first_grad, axis=0)
        first_low = first_grad.astype(jnp.bfloat16)
        out_step = contract_rows(first_low, attended_low)
        attended_grad = jnp.dot(first_low, full_out, preferred_element_type=jnp.float32)
        attended_grad = attended_grad.astype(jnp.bfloat16).reshape(
            seq_local, rows_local, heads_local, HD
        )
        scores = masked_scores(queries, key_rows, same_segment, score_scale)
        probabilities = jnp.exp(scores - log_total)
        value_grad = jnp.einsum(
            "shqk,sqhe->skhe",
            probabilities.astype(jnp.bfloat16),
            attended_grad,
            preferred_element_type=jnp.float32,
        )
        prob_grad = jnp.einsum(
            "sqhe,skhe->shqk", attended_grad, value_rows, preferred_element_type=jnp.float32
        )
        row_dot = jnp.sum(prob_grad * probabilities, axis=-1, keepdims=True)
        score_grad = (probabilities * (prob_grad - row_dot)).astype(jnp.bfloat16)
        query_grad = (
            jnp.einsum("shqk,skhe->sqhe", score_grad, key_rows, preferred_element_type=jnp.float32)
            * score_scale
        )
        key_grad = (
            jnp.einsum("shqk,sqhe->skhe", score_grad, queries, preferred_element_type=jnp.float32)
            * score_scale
        )
        kv_grads = lax.psum_scatter(
            jnp.concatenate([key_grad, value_grad], axis=-1).astype(jnp.bfloat16),
            "ctx",
            scatter_dimension=1,
            tiled=True,
        ).astype(jnp.float32)
        key_mine = kv_grads[..., :HD]
        value_mine = kv_grads[..., HD:]
        bias_step = jnp.stack(
            [jnp.sum(query_grad, axis=(0, 1)), jnp.sum(value_mine, axis=(0, 1))], axis=1
        )
        qv_bias_grad = qv_bias_grad + bias_step.reshape(-1)
        mixed_grad = jnp.stack([query_grad, key_mine, value_mine], axis=3)
        mixed_grad = mixed_grad.reshape(tokens, 3 * heads_local * HD).astype(jnp.bfloat16)
        qkv_step = contract_rows(x_low, mixed_grad)
        input_part = times_transposed(mixed_grad, full_qkv).reshape(
            seq_local, rows_local, model_width
        )
        input_mine = lax.psum_scatter(
            input_part.astype(jnp.bfloat16), "tp", scatter_dimension=1, tiled=True
        ).astype(jnp.float32)
        first_part = pick_rows(first_grad)
        input_rows.append(input_mine + first_part)
        gain_step = jnp.stack([gain_one, gain_two], axis=1)
        shift_step = jnp.stack([shift_zero, shift_one, shift_two, shift_three], axis=1)
        full_totals = tuple(
            map(
                add_pair,
                full_totals,
                (qkv_step, out_step, up_step, down_step, gain_step, shift_step),
            )
        )
    share_totals = (
        lax.psum_scatter(
            full_totals[0].astype(jnp.bfloat16), ("fsdp", "ctx"), scatter_dimension=0, tiled=True
        ).astype(jnp.float32),
        lax.psum_scatter(
            full_totals[1].astype(jnp.bfloat16), ("fsdp", "ctx"), scatter_dimension=0, tiled=True
        ).astype(jnp.float32),
        lax.psum_scatter(
            full_totals[2].astype(jnp.bfloat16), ("fsdp", "ctx"), scatter_dimension=0, tiled=True
        ).astype(jnp.float32),
        lax.psum_scatter(
            full_totals[3].astype(jnp.bfloat16), ("fsdp", "ctx"), scatter_dimension=0, tiled=True
        ).astype(jnp.float32),
        lax.psum_scatter(
            full_totals[4].astype(jnp.bfloat16), ("fsdp", "ctx"), scatter_dimension=0, tiled=True
        ).astype(jnp.float32),
        lax.psum_scatter(
            full_totals[5].astype(jnp.bfloat16), ("fsdp", "ctx"), scatter_dimension=0, tiled=True
        ).astype(jnp.float32),
    )
    qv_total, up_total = lax.psum((qv_bias_grad, up_bias_grad), ("fsdp", "ctx"))
    return (
        jnp.stack(layer_rows, axis=0),
        jnp.stack(input_rows, axis=0),
        share_totals[0],
        qv_total,
        share_totals[1],
        share_totals[2],
        up_total,
        share_totals[3],
        share_totals[4],
        share_totals[5],
    )


def solution(mesh):
    placed = (
        P(None, "fsdp", "ctx", None),
        P(None, "fsdp", "ctx", None),
        P(None, "fsdp", None),
        P(("fsdp", "ctx"), "tp"),
        P("tp"),
        P(("fsdp", "ctx"), "tp"),
        P(("fsdp", "ctx"), "tp"),
        P("tp"),
        P(("fsdp", "ctx"), "tp"),
        P(("fsdp", "ctx"), None),
        P(("fsdp", "ctx"), None),
    )
    return jax.shard_map(
        local,
        mesh=mesh,
        in_specs=placed,
        out_specs=(
            P(None, "fsdp", ("ctx", "tp"), None),
            P(None, "fsdp", ("ctx", "tp"), None),
            P(("fsdp", "ctx"), "tp"),
            P("tp"),
            P(("fsdp", "ctx"), "tp"),
            P(("fsdp", "ctx"), "tp"),
            P("tp"),
            P(("fsdp", "ctx"), "tp"),
            P(("fsdp", "ctx"), None),
            P(("fsdp", "ctx"), None),
        ),
        check_vma=False,
    )
```

profile of v0, /device:TPU:0, one launch (start us, length us, event | category | flops | bytes accessed | tf_op | source)
XLA Modules:
  0.0 1028.2 jit_solution(4687349844855321863)
XLA Ops:
  9.5 28.8 %all-gather.6.cloned.1.call-done = bf16[1024,768]{1,0:T(8,128)(2,1)} async-done(((bf16[128,768]{1,0:T(8,128)(2,1)}), bf16[1024,768]{1,0:T(8,128)(2,1)}) %all-gather.6.cloned.1.call-update) | async-done | bytes 1572880 | tf_op jit(solution)/shard_map/all_gather | solution.py:89
  38.2 2.6 copy.51
  40.8 2.6 fusion.38
  45.8 19.5 %all_gather.32 = bf16[1024,256]{1,0:T(8,128)(2,1)S(1)} all-gather(bf16[128,256]{1,0:T(8,128)(2,1)S(1)} %copy-done.39), channel_id=1, replica_groups=mesh['fsdp'=4,'ctx'=2,'tp'=4] {'fsdp','ctx'}, dimensions={0}, use_global_device_ids=true | all-gather | bytes 589824 | tf_op jit(solution)/shard_map/all_gather | solution.py:90
  67.8 2.2 all-gather.8.cloned.1.call-done
  70.0 2.2 fusion.143
  75.9 17.4 %all-gather.14.cloned.1.call-done = bf16[2,512,4,128]{1,3,2,0:T(8,128)(2,1)} async-done(((bf16[2,256,4,128]{1,3,2,0:T(8,128)(2,1)}), bf16[2,512,4,128]{1,3,2,0:T(8,128)(2,1)}) %all-gather.14.cloned.1.call-update) | async-done | bytes 1048592 | tf_op jit(solution)/shard_map/all_gather | solution.py:107
  93.4 2.3 fusion.144
  99.5 1.8 fusion.147
  101.3 1.8 fusion.149
  106.2 12.1 %all_gather.33 = bf16[1024,4]{0,1:T(4,128)(2,1)S(1)} all-gather(bf16[128,4]{0,1:T(4,128)(2,1)S(1)} %copy-done.41), channel_id=1, replica_groups=mesh['fsdp'=4,'ctx'=2,'tp'=4] {'fsdp','ctx'}, dimensions={0}, use_global_device_ids=true | all-gather | bytes 9216 | tf_op jit(solution)/shard_map/all_gather | solution.py:94
  118.4 10.9 %all_gather.34 = bf16[1024,2]{0,1:T(2,128)(2,1)S(1)} all-gather(bf16[128,2]{0,1:T(2,128)(2,1)S(1)} %copy-done.42), channel_id=1, replica_groups=mesh['fsdp'=4,'ctx'=2,'tp'=4] {'fsdp','ctx'}, dimensions={0}, use_global_device_ids=true | all-gather | bytes 4608 | tf_op jit(solution)/shard_map/all_gather | solution.py:93
  129.3 129.0 %all-reduce.12.cloned.1.call-done = (f32[512,1024]{1,0:T(8,128)}, f32[512,1024]{1,0:T(8,128)}) async-done(((f32[512,1024]{1,0:T(8,128)}, f32[512,1024]{1,0:T(8,128)}), (f32[512,1024]{1,0:T(8,128)}, f32[512,1024]{1,0:T(8,128)})) %all-reduce.12.cloned.1.call-update) | async-done | bytes 4194320 | tf_op jit(solution)/shard_map/psum | solution.py:47
  258.3 3.4 fusion.135
  263.1 23.7 %all-gather.10.cloned.1.call-done = bf16[1024,1024]{1,0:T(8,128)(2,1)} async-done(((bf16[128,1024]{1,0:T(8,128)(2,1)}), bf16[1024,1024]{1,0:T(8,128)(2,1)}) %all-gather.10.cloned.1.call-update) | async-done | bytes 2097168 | tf_op jit(solution)/shard_map/all_gather | solution.py:91
  286.8 3.7 fusion.124
  291.9 11.7 %multiply_convert_fusion.2 = (bf16[512,1024]{1,0:T(8,128)(2,1)}, f32[512,1024]{1,0:T(8,128)}, bf16[512,1024]{1,0:T(8,128)(2,1)}, f32[512,1024]{1,0:T(8,128)}, f32[512,1024]{1,0:T(8,128)}) fusion(f32[1024]{0:T(1024)S(1)} %convert_element_type.236, f32[512,1024]{1,0:T(8,128)S(1)} %fusion.124, bf16[1024,1024]{1,0:T(8,128)(2,1)S(1)} %copy-done.43, ...), kind=kOutput, calls=%fused_computation.54 | convolution fusion | flops 1145569280 | bytes 14696448 | tf_op jit(solution)/shard_map/dot_general | solution.py:129
  303.6 12.8 %all-gather.12.cloned.1.call-done = bf16[1024,1024]{1,0:T(8,128)(2,1)} async-done(((bf16[128,1024]{1,0:T(8,128)(2,1)}), bf16[1024,1024]{1,0:T(8,128)(2,1)}) %all-gather.12.cloned.1.call-update) | async-done | bytes 2097168 | tf_op jit(solution)/shard_map/all_gather | solution.py:92
  316.4 4.7 fusion.148
  321.1 2.6 fusion.150
  324.2 154.7 %all-reduce.10.cloned.1.call-done = (f32[512,1024]{1,0:T(8,128)}, f32[512,1024]{1,0:T(8,128)}) async-done(((f32[512,1024]{1,0:T(8,128)}, f32[512,1024]{1,0:T(8,128)}), (f32[512,1024]{1,0:T(8,128)}, f32[512,1024]{1,0:T(8,128)})) %all-reduce.10.cloned.1.call-update) | async-done | bytes 4194320 | tf_op jit(solution)/shard_map/psum | solution.py:47
  478.9 4.2 fusion.132
  483.8 1.6 copy-done.15
  485.4 1.8 fusion.17
  487.2 1.7 fusion.130
  490.4 2.0 fusion.145
  492.4 2.6 fusion.89
  495.8 2.0 fusion.146
  498.7 2.7 fusion.82
  501.7 153.9 %all-reduce.8.cloned.1.call-done = (f32[512,1024]{1,0:T(8,128)}, f32[512,1024]{1,0:T(8,128)}) async-done(((f32[512,1024]{1,0:T(8,128)}, f32[512,1024]{1,0:T(8,128)}), (f32[512,1024]{1,0:T(8,128)}, f32[512,1024]{1,0:T(8,128)})) %all-reduce.8.cloned.1.call-update) | async-done | bytes 4194320 | tf_op jit(solution)/shard_map/psum | solution.py:47
  655.6 4.0 multiply_reduce_fusion.2
  660.9 1.9 multiply_reduce_fusion.3
  663.5 1.7 fusion.126
  669.3 3.2 fusion.56
  672.8 2.5 multiply_reduce_fusion
  680.3 2.0 convolution_convert_fusion.1
  682.9 4.0 multiply_reduce_fusion.1
  687.9 2.0 fusion.63
  692.0 3.4 fusion.87
  695.5 2.9 add_convert_fusion.1
  698.6 3.4 fusion.115
  702.0 2.8 add_convert_fusion
  704.9 1.9 convert_reduce_fusion
  707.7 2.1 fusion.84
  710.9 2.9 fusion.49
  713.8 2.6 bitcast_reduce_fusion
  719.4 2.0 fusion.43
  721.6 2.6 bitcast_reduce_fusion.1
  727.4 2.0 fusion.40
  729.7 1.9 copy.68
  734.3 2.2 fusion.46
  736.4 2.6 copy.77
  739.1 2.3 multiply_add_fusion.4
  742.3 24.5 %reduce-scatter.27.cloned.1.call-done = bf16[128,1024]{1,0:T(8,128)(2,1)} async-done(((bf16[1024,1024]{1,0:T(8,128)(2,1)}), bf16[128,1024]{1,0:T(8,128)(2,1)}) %reduce-scatter.27.cloned.1.call-update) | async-done | bytes 262160 | tf_op jit(solution)/shard_map/reduce_scatter | solution.py:217
  766.7 1.8 convert_element_type.284
  768.5 42.5 %reduce-scatter.29.cloned.1.call-done = bf16[128,1024]{1,0:T(8,128)(2,1)} async-done(((bf16[1024,1024]{1,0:T(8,128)(2,1)}), bf16[128,1024]{1,0:T(8,128)(2,1)}) %reduce-scatter.29.cloned.1.call-update) | async-done | bytes 262160 | tf_op jit(solution)/shard_map/reduce_scatter | solution.py:220
  811.0 1.8 convert_element_type.286
  812.8 35.0 %reduce-scatter.33.cloned.1.call-done = bf16[128,2]{1,0:T(8,128)(2,1)} async-done(((bf16[1024,2]{1,0:T(8,128)(2,1)}), bf16[128,2]{1,0:T(8,128)(2,1)}) %reduce-scatter.33.cloned.1.call-update) | async-done | bytes 528
  849.2 35.2 %reduce-scatter.35.cloned.1.call-done = bf16[128,4]{1,0:T(8,128)(2,1)} async-done(((bf16[1024,4]{1,0:T(8,128)(2,1)}), bf16[128,4]{1,0:T(8,128)(2,1)}) %reduce-scatter.35.cloned.1.call-update) | async-done | bytes 1040
  885.8 35.7 %reduce-scatter.25.cloned.1.call-done = bf16[128,256]{1,0:T(8,128)(2,1)} async-done(((bf16[1024,256]{1,0:T(8,128)(2,1)}), bf16[128,256]{1,0:T(8,128)(2,1)}) %reduce-scatter.25.cloned.1.call-update) | async-done | bytes 65552 | tf_op jit(solution)/shard_map/reduce_scatter | solution.py:214
  923.3 14.3 %all-reduce = (f32[512]{0:T(512)}, f32[1024]{0:T(1024)}) all-reduce(f32[512]{0:T(512)S(1)} %add.309, f32[1024]{0:T(1024)S(1)} %add.312), channel_id=1, replica_groups=mesh['fsdp'=4,'ctx'=2,'tp'=4] {'fsdp','ctx'}, use_global_device_ids=true, to_apply=%region_37.38 | all-reduce | flops 1536 | bytes 12288 | tf_op jit(solution)/shard_map/psum | solution.py:230
  937.6 13.3 %reduce-scatter.23.cloned.1.call-done = bf16[2,64,1024]{2,1,0:T(8,128)(2,1)} async-done(((bf16[2,256,1024]{2,1,0:T(8,128)(2,1)}), bf16[2,64,1024]{2,1,0:T(8,128)(2,1)}) %reduce-scatter.23.cloned.1.call-update) | async-done | bytes 262160 | tf_op jit(solution)/shard_map/reduce_scatter | solution.py:196
  952.1 26.8 %reduce-scatter.19.cloned.1.call-done = bf16[2,64,1024]{2,1,0:T(8,128)(2,1)} async-done(((bf16[2,256,1024]{2,1,0:T(8,128)(2,1)}), bf16[2,64,1024]{2,1,0:T(8,128)(2,1)}) %reduce-scatter.19.cloned.1.call-update) | async-done | bytes 262160 | tf_op jit(solution)/shard_map/reduce_scatter | solution.py:196
  981.1 37.8 %reduce-scatter.31.cloned.1.call-done = bf16[128,768]{1,0:T(8,128)(2,1)} async-done(((bf16[1024,768]{1,0:T(8,128)(2,1)}), bf16[128,768]{1,0:T(8,128)(2,1)}) %reduce-scatter.31.cloned.1.call-update) | async-done | bytes 196624
  (239 shorter events, 61.8 us)
Async XLA Ops:
  7.2 33.6 %copy-start.31 = (bf16[2,2,256,1024]{3,2,1,0:T(8,128)(2,1)S(1)}, bf16[2,2,256,1024]{3,2,1,0:T(8,128)(2,1)}, u32[]{:S(2)}) copy-start(bf16[2,2,256,1024]{3,2,1,0:T(8,128)(2,1)} %param.11) | copy-start | bytes 6291460
  7.2 31.0 %all-gather.6.cloned.1.call-start = ((), (), s32[]{:S(2)}) async-start(), calls=%async_computation.10 | async-start | bytes 1769472 | tf_op jit(solution)/shard_map/all_gather | solution.py:89
  7.9 62.1 %all-gather.8.cloned.1.call-start = ((), (), s32[]{:S(2)}) async-start(), calls=%async_computation.11 | async-start | bytes 1572864 | tf_op jit(solution)/shard_map/all_gather | solution.py:107
  40.8 2.6 copy-start.32
  40.8 2.6 copy-start.36
  44.4 25.5 %copy-start.28 = (f32[2,256,4,3,64]{1,4,3,2,0:T(8,128)}, f32[2,256,4,3,64]{1,4,3,2,0:T(8,128)S(1)}, u32[]{:S(2)}) copy-start(f32[2,256,4,3,64]{1,4,3,2,0:T(8,128)S(1)} %fusion.69) | copy-start | bytes 4718596
  44.4 1.4 copy-start.39
  45.8 47.6 %all-gather.14.cloned.1.call-start = ((), (), s32[]{:S(2)}) async-start(), calls=%async_computation.14 | async-start | bytes 1572864 | tf_op jit(solution)/shard_map/all_gather | solution.py:107
  67.7 190.6 %all-reduce.12.cloned.1.call-start = ((), (), s32[]{:S(2)}) async-start(), calls=%async_computation.27 | async-start | bytes 8388608 | tf_op jit(solution)/shard_map/psum | solution.py:47
  72.2 1.9 copy-start
  72.2 2.0 copy-start.25
  95.7 2.0 copy-start.2
  95.7 2.0 copy-start.26
  99.5 3.6 copy-start.27
  103.1 1.6 copy-start.33
  103.1 183.7 %all-gather.10.cloned.1.call-start = ((), (), s32[]{:S(2)}) async-start(), calls=%async_computation.12 | async-start | bytes 2359296 | tf_op jit(solution)/shard_map/all_gather | solution.py:91
  103.7 212.7 %all-gather.12.cloned.1.call-start = ((), (), s32[]{:S(2)}) async-start(), calls=%async_computation.13 | async-start | bytes 2359296 | tf_op jit(solution)/shard_map/all_gather | solution.py:92
  104.3 1.9 copy-start.41
  104.3 14.0 %copy-start.40 = (bf16[1024]{0:T(1024)(128)(2,1)S(1)}, bf16[1024]{0:T(1024)(128)(2,1)}, u32[]{:S(2)}) copy-start(bf16[1024]{0:T(1024)(128)(2,1)} %param.18) | copy-start | bytes 6148
  104.3 14.0 %copy-start.42 = (bf16[128,2]{0,1:T(2,128)(2,1)S(1)}, bf16[128,2]{0,1:T(2,128)(2,1)}, u32[]{:S(2)}) copy-start(bf16[128,2]{0,1:T(2,128)(2,1)} %param.20) | copy-start | bytes 1540
  104.3 374.5 %all-reduce.10.cloned.1.call-start = ((), (), s32[]{:S(2)}) async-start(), calls=%async_computation.26 | async-start | bytes 8388608 | tf_op jit(solution)/shard_map/psum | solution.py:47
  261.7 28.8 %copy-start.5 = (f32[512,1024]{1,0:T(8,128)}, f32[512,1024]{1,0:T(8,128)S(1)}, u32[]{:S(2)}) copy-start(f32[512,1024]{1,0:T(8,128)S(1)} %get-tuple-element.83) | copy-start | bytes 6291460
  286.8 5.0 copy-start.43
  290.5 1.4 copy-start.52
  316.4 4.7 copy-start.37
  316.4 4.7 copy-start.45
  323.7 331.9 %all-reduce.8.cloned.1.call-start = ((), (), s32[]{:S(2)}) async-start(), calls=%async_computation.25 | async-start | bytes 8388608 | tf_op jit(solution)/shard_map/psum | solution.py:47
  483.1 4.2 copy-start.4
  483.1 2.3 copy-start.15
  487.2 1.8 copy-start.46
  487.2 2.2 copy-start.53
  487.2 3.2 copy-start.54
  488.9 3.4 copy-start.10
  489.0 6.1 copy-start.13
  490.4 2.0 copy-start.44
  492.4 2.6 copy-start.49
  492.4 2.6 copy-start.50
  492.4 3.3 copy-start.51
  501.4 215.0 %reduce-scatter.21.cloned.1.call-start = ((), (), s32[]{:S(2)}) async-start(), calls=%async_computation.17 | async-start | bytes 1572864 | tf_op jit(solution)/shard_map/reduce_scatter | solution.py:178
  655.6 4.1 copy-start.6
  655.6 4.1 copy-start.9
  655.6 4.7 copy-start.11
  655.6 5.3 copy-start.30
  665.2 1.4 copy-start.12
  669.3 3.5 copy-start.3
  680.3 44.0 %reduce-scatter.17.cloned.1.call-start = ((), (), s32[]{:S(2)}) async-start(), calls=%async_computation.15 | async-start | bytes 1572864 | tf_op jit(solution)/shard_map/reduce_scatter | solution.py:178
  682.9 4.0 copy-start.1
  687.8 2.8 copy-start.17
  691.8 3.7 copy-start.48
  691.8 75.0 %reduce-scatter.27.cloned.1.call-start = ((), (), s32[]{:S(2)}) async-start(), calls=%async_computation.20 | async-start | bytes 2359296 | tf_op jit(solution)/shard_map/reduce_scatter | solution.py:217
  692.0 3.5 copy-start.7
  698.5 3.5 copy-start.38
  698.5 112.5 %reduce-scatter.29.cloned.1.call-start = ((), (), s32[]{:S(2)}) async-start(), calls=%async_computation.21 | async-start | bytes 2359296 | tf_op jit(solution)/shard_map/reduce_scatter | solution.py:220
  698.5 3.4 copy-start.14
  704.9 142.9 %reduce-scatter.33.cloned.1.call-start = ((), (), s32[]{:S(2)}) async-start(), calls=%async_computation.23 | async-start | bytes 294912
  709.8 174.5 %reduce-scatter.35.cloned.1.call-start = ((), (), s32[]{:S(2)}) async-start(), calls=%async_computation.24 | async-start | bytes 294912
  710.8 210.6 %reduce-scatter.25.cloned.1.call-start = ((), (), s32[]{:S(2)}) async-start(), calls=%async_computation.19 | async-start | bytes 589824 | tf_op jit(solution)/shard_map/reduce_scatter | solution.py:214
  713.8 237.1 %reduce-scatter.23.cloned.1.call-start = ((), (), s32[]{:S(2)}) async-start(), calls=%async_computation.18 | async-start | bytes 1310720 | tf_op jit(solution)/shard_map/reduce_scatter | solution.py:196
  717.6 1.8 copy-start.34
  721.5 257.3 %reduce-scatter.19.cloned.1.call-start = ((), (), s32[]{:S(2)}) async-start(), calls=%async_computation.16 | async-start | bytes 1310720 | tf_op jit(solution)/shard_map/reduce_scatter | solution.py:196
  725.4 2.0 copy-start.35
  729.4 289.4 %reduce-scatter.31.cloned.1.call-start = ((), (), s32[]{:S(2)}) async-start(), calls=%async_computation.22 | async-start | bytes 1769472
  741.4 181.6 %copy-start.24 = (f32[2,256,4,128]{1,3,2,0:T(8,128)S(1)}, f32[2,256,4,128]{1,3,2,0:T(8,128)}, u32[]{:S(2)}) copy-start(f32[2,256,4,128]{1,3,2,0:T(8,128)} %copy-done.23) | copy-start | bytes 3145732
  741.4 181.7 %copy-start.22 = (f32[2,256,4,128]{1,3,2,0:T(8,128)S(1)}, f32[2,256,4,128]{1,3,2,0:T(8,128)}, u32[]{:S(2)}) copy-start(f32[2,256,4,128]{1,3,2,0:T(8,128)} %copy-done.21) | copy-start | bytes 3145732
  (9 other events, 10.3 us)
Sparse Core Ops, SparseCore 0:
  9.9 28.2 all-gather.5
  45.9 24.0 all-gather.7
  72.1 21.2 all-gather.13
  103.3 155.0 all-reduce.11
  260.1 26.7 all-gather.9
  288.6 27.7 all-gather.11
  323.8 155.0 all-reduce.9
  501.6 153.9 all-reduce.7
  680.4 19.3 reduce-scatter.20
  701.9 20.3 reduce-scatter.16
  725.6 41.1 reduce-scatter.26
  769.9 41.0 reduce-scatter.28
  814.0 33.6 reduce-scatter.32
  850.6 33.6 reduce-scatter.34
  887.3 34.1 reduce-scatter.24
  923.6 27.2 reduce-scatter.22
  953.0 25.7 reduce-scatter.18
  982.0 36.8 reduce-scatter.30
where the time goes:
time: 1040 us; the launch traced here: 1030 us
  waiting for transfers between devices  775 us (75%)
  matrix products  93.1 us (9%)
  blocking collectives  56.8 us (5%)
  other arithmetic  47.2 us (5%)
  local copies, waits for them, and re-layouts  38.3 us (4%)
  between operations  15.8 us (2%)
    psum x3, waiting for transfers between devices, reduce_rows(): return lax.psum(part, 'tp')  438 us
    unnamed x21, waiting for transfers between devices  110 us
    reduce_scatter x1, waiting for transfers between devices, local(): lax.psum_scatter(full_totals[3].astype(jnp.bfloat16), ('fsdp', 'ctx'), sc...  42.5 us
    reduce_scatter x2, waiting for transfers between devices, local(): lax.psum_scatter(input_part.astype(jnp.bfloat16), 'tp', scatter_dimension...  40.1 us
    reduce_scatter x1, waiting for transfers between devices, local(): lax.psum_scatter(full_totals[1].astype(jnp.bfloat16), ('fsdp', 'ctx'), sc...  35.7 us
    all_gather x1, waiting for transfers between devices, local(): lax.all_gather(w_qkv, ('fsdp', 'ctx'), axis=0, tiled=True)  28.8 us
    unnamed x121, local copies, waits for them, and re-layouts  25.1 us
    reduce_scatter x1, waiting for transfers between devices, local(): lax.psum_scatter(full_totals[2].astype(jnp.bfloat16), ('fsdp', 'ctx'), sc...  24.5 us
  transfers between devices with their start and end apart: 18, of which 16 were waited for; matrix products, arithmetic and copies ran while one was open for 10% of the time, Pallas kernels for 0%

commit v1 on v0

--- a/solution.py
+++ b/solution.py
@@ -6,6 +6,27 @@
 HD = 64
 norm_epsilon = 1e-12
 masked_score = -1e30
+
+
+def collect(shard, axis, dim):
+    size, place, width = (lax.axis_size(axis), lax.axis_index(axis), shard.shape[dim])
+    right = [(i, (i + 1) % size) for i in range(size)]
+    backward = [(i, (i - 1) % size) for i in range(size)]
+    out = jnp.zeros((*shard.shape[:dim], size * width, *shard.shape[dim + 1 :]), shard.dtype)
+    out = lax.dynamic_update_slice_in_dim(out, shard, place * width, axis=dim)
+    from_left = from_right = shard
+    halfway = size // 2
+    for step in range(1, halfway + 1):
+        from_left = lax.ppermute(from_left, axis, right)
+        out = lax.dynamic_update_slice_in_dim(
+            out, from_left, (place - step) % size * width, axis=dim
+        )
+        if step < size - halfway:
+            from_right = lax.ppermute(from_right, axis, backward)
+            out = lax.dynamic_update_slice_in_dim(
+                out, from_right, (place + step) % size * width, axis=dim
+            )
+    return out
 
 
 def norm_rows(rows_in, gain_row, offset):
@@ -86,7 +107,7 @@
     input_rows = []
     for batch_index in range(batches):
         gathered = (
-            lax.all_gather(w_qkv, ("fsdp", "ctx"), axis=0, tiled=True),
+            collect(w_qkv, ("fsdp", "ctx"), 0),
             lax.all_gather(w_out, ("fsdp", "ctx"), axis=0, tiled=True),
             lax.all_gather(w_up, ("fsdp", "ctx"), axis=0, tiled=True),
             lax.all_gather(w_down, ("fsdp", "ctx"), axis=0, tiled=True),

time: 1040 us -> 1010 us (0.971)
  waiting for transfers between devices: 775 us -> 718 us
  starting transfers between devices: 1.78 us -> 18.3 us
    all_gather x1 -> x0, waiting for transfers between devices: 28.8 us -> none  [local(): lax.all_gather(w_qkv, ('fsdp', 'ctx'), axis=0, tiled=True)]
    all_gather x1, waiting for transfers between devices: 23.7 us -> 0.01 us  [local(): lax.all_gather(w_up, ('fsdp', 'ctx'), axis=0, tiled=True)]
    ppermute x0 -> x7, starting transfers between devices: none -> 16.3 us  [the longest x4 10.4 us: collect(): from_left = lax.ppermute(from_left, axis, right)]
    all_gather x1, waiting for transfers between devices: 12.8 us -> 0.01 us  [local(): lax.all_gather(w_down, ('fsdp', 'ctx'), axis=0, tiled=True)]
    unnamed x121 -> x131, local copies, waits for them, and re-layouts: 25.1 us -> 24.6 us
    unnamed x21 -> x20, waiting for transfers between devices: 110 us -> 110 us
  transfers between devices with their start and end apart: 18 -> 24, of which waited for: 16 -> 18; matrix products, arithmetic and copies ran while one was open for 10% -> 11% of each run, Pallas kernels for 0% -> 0%
where the time goes in v1:
time: 1010 us; the launch traced here: 1000 us
  waiting for transfers between devices  718 us (71%)
  matrix products  97 us (10%)
  blocking collectives  57.5 us (6%)
  other arithmetic  48.4 us (5%)
  local copies, waits for them, and re-layouts  48.1 us (5%)
  starting transfers between devices  18.3 us (2%)
  between operations  16.7 us (2%)
    psum x3, waiting for transfers between devices, reduce_rows(): return lax.psum(part, 'tp')  438 us
    unnamed x20, waiting for transfers between devices  110 us
    reduce_scatter x1, waiting for transfers between devices, local(): lax.psum_scatter(full_totals[3].astype(jnp.bfloat16), ('fsdp', 'ctx'), sc...  42.7 us
    reduce_scatter x2, waiting for transfers between devices, local(): lax.psum_scatter(input_part.astype(jnp.bfloat16), 'tp', scatter_dimension...  40.2 us
    reduce_scatter x1, waiting for transfers between devices, local(): lax.psum_scatter(full_totals[1].astype(jnp.bfloat16), ('fsdp', 'ctx'), sc...  35.7 us
    unnamed x131, local copies, waits for them, and re-layouts  24.6 us
    dot_general x8, matrix products, times_transposed(): lax.dot_general(left_rows, right_rows, (((1,), (1,)), ((), ())), preferre...  23.1 us
    reduce_scatter x1, waiting for transfers between devices, local(): lax.psum_scatter(full_totals[2].astype(jnp.bfloat16), ('fsdp', 'ctx'), sc...  22.2 us
  transfers between devices with their start and end apart: 24, of which 18 were waited for; matrix products, arithmetic and copies ran while one was open for 11% of the time, Pallas kernels for 0%

profile of v1, /device:TPU:0, one launch (start us, length us, event | category | flops | bytes accessed | tf_op | source)
XLA Modules:
  0.0 1004.2 jit_solution(1088559569363354977)
XLA Ops:
  8.1 3.0 collective-permute-start
  16.7 2.4 collective-permute-start.2
  19.1 1.8 collective-permute-done.1
  20.9 2.7 collective-permute-start.3
  25.0 2.5 collective-permute-start.4
  29.2 2.8 collective-permute-start.5
  33.4 2.5 collective-permute-start.6
  38.3 3.4 collective-permute-done.6
  42.4 3.6 convolution_bitcast_fusion.1
  46.0 2.3 reshape.256
  49.6 3.6 convolution_bitcast_fusion
  53.2 2.3 reshape.260
  58.3 19.9 %all_gather.27 = bf16[1024,256]{1,0:T(8,128)(2,1)S(1)} all-gather(bf16[128,256]{1,0:T(8,128)(2,1)S(1)} %copy-done.41), channel_id=1, replica_groups=mesh['fsdp'=4,'ctx'=2,'tp'=4] {'fsdp','ctx'}, dimensions={0}, use_global_device_ids=true | all-gather | bytes 589824 | tf_op jit(solution)/shard_map/all_gather | solution.py:111
  80.7 2.9 all-gather.5.cloned.1.call-done
  83.7 2.2 fusion.140
  89.6 17.4 %all-gather.11.cloned.1.call-done = bf16[2,512,4,128]{1,3,2,0:T(8,128)(2,1)} async-done(((bf16[2,256,4,128]{1,3,2,0:T(8,128)(2,1)}), bf16[2,512,4,128]{1,3,2,0:T(8,128)(2,1)}) %all-gather.11.cloned.1.call-update) | async-done | bytes 1048592 | tf_op jit(solution)/shard_map/all_gather | solution.py:128
  107.0 2.2 fusion.141
  113.0 1.8 fusion.144
  117.9 12.3 %all_gather.28 = bf16[1024,4]{0,1:T(4,128)(2,1)S(1)} all-gather(bf16[128,4]{0,1:T(4,128)(2,1)S(1)} %copy-done.45), channel_id=1, replica_groups=mesh['fsdp'=4,'ctx'=2,'tp'=4] {'fsdp','ctx'}, dimensions={0}, use_global_device_ids=true | all-gather | bytes 9216 | tf_op jit(solution)/shard_map/all_gather | solution.py:115
  130.2 11.0 %all_gather.29 = bf16[1024,2]{0,1:T(2,128)(2,1)S(1)} all-gather(bf16[128,2]{0,1:T(2,128)(2,1)S(1)} %copy-done.46), channel_id=1, replica_groups=mesh['fsdp'=4,'ctx'=2,'tp'=4] {'fsdp','ctx'}, dimensions={0}, use_global_device_ids=true | all-gather | bytes 4608 | tf_op jit(solution)/shard_map/all_gather | solution.py:114
  141.2 130.6 %all-reduce.12.cloned.1.call-done = (f32[512,1024]{1,0:T(8,128)}, f32[512,1024]{1,0:T(8,128)}) async-done(((f32[512,1024]{1,0:T(8,128)}, f32[512,1024]{1,0:T(8,128)}), (f32[512,1024]{1,0:T(8,128)}, f32[512,1024]{1,0:T(8,128)})) %all-reduce.12.cloned.1.call-update) | async-done | bytes 4194320 | tf_op jit(solution)/shard_map/psum | solution.py:68
  271.9 3.5 fusion.130
  276.7 3.7 fusion.119
  281.8 11.7 %multiply_convert_fusion.2 = (bf16[512,1024]{1,0:T(8,128)(2,1)}, f32[512,1024]{1,0:T(8,128)}, bf16[512,1024]{1,0:T(8,128)(2,1)}, f32[512,1024]{1,0:T(8,128)}, f32[512,1024]{1,0:T(8,128)}) fusion(f32[1024]{0:T(1024)S(1)} %convert_element_type.236, f32[512,1024]{1,0:T(8,128)S(1)} %fusion.119, bf16[1024,1024]{1,0:T(8,128)(2,1)S(1)} %copy-done.47, ...), kind=kOutput, calls=%fused_computation.54 | convolution fusion | flops 1145569280 | bytes 14696448 | tf_op jit(solution)/shard_map/dot_general | solution.py:150
  293.5 4.7 fusion.145
  298.2 2.6 fusion.147
  301.1 153.8 %all-reduce.10.cloned.1.call-done = (f32[512,1024]{1,0:T(8,128)}, f32[512,1024]{1,0:T(8,128)}) async-done(((f32[512,1024]{1,0:T(8,128)}, f32[512,1024]{1,0:T(8,128)}), (f32[512,1024]{1,0:T(8,128)}, f32[512,1024]{1,0:T(8,128)})) %all-reduce.10.cloned.1.call-update) | async-done | bytes 4194320 | tf_op jit(solution)/shard_map/psum | solution.py:68
  455.0 4.2 fusion.127
  466.5 2.0 fusion.142
  468.5 2.6 fusion.84
  471.9 2.0 fusion.143
  474.8 2.7 fusion.77
  478.1 153.6 %all-reduce.8.cloned.1.call-done = (f32[512,1024]{1,0:T(8,128)}, f32[512,1024]{1,0:T(8,128)}) async-done(((f32[512,1024]{1,0:T(8,128)}, f32[512,1024]{1,0:T(8,128)}), (f32[512,1024]{1,0:T(8,128)}, f32[512,1024]{1,0:T(8,128)})) %all-reduce.8.cloned.1.call-update) | async-done | bytes 4194320 | tf_op jit(solution)/shard_map/psum | solution.py:68
  631.7 4.0 multiply_reduce_fusion.2
  637.0 1.9 multiply_reduce_fusion.3
  645.4 3.2 fusion.54
  648.8 2.5 multiply_reduce_fusion
  655.4 2.0 convolution_convert_fusion.1
  659.7 4.1 multiply_reduce_fusion.1
  667.5 3.4 fusion.82
  671.0 2.9 add_convert_fusion.1
  674.0 3.4 fusion.112
  677.4 2.8 add_convert_fusion
  680.4 1.9 convert_reduce_fusion
  683.1 2.1 fusion.79
  686.3 2.9 fusion.47
  689.3 2.6 bitcast_reduce_fusion
  694.1 3.5 fusion.41
  697.6 2.6 bitcast_reduce_fusion.1
  703.5 3.4 fusion.38
  707.2 2.0 copy.113
  711.7 2.2 fusion.44
  713.9 2.6 copy.118
  716.5 2.3 multiply_add_fusion.4
  719.7 22.2 %reduce-scatter.27.cloned.1.call-done = bf16[128,1024]{1,0:T(8,128)(2,1)} async-done(((bf16[1024,1024]{1,0:T(8,128)(2,1)}), bf16[128,1024]{1,0:T(8,128)(2,1)}) %reduce-scatter.27.cloned.1.call-update) | async-done | bytes 262160 | tf_op jit(solution)/shard_map/reduce_scatter | solution.py:238
  741.9 1.8 convert_element_type.284
  743.7 42.7 %reduce-scatter.29.cloned.1.call-done = bf16[128,1024]{1,0:T(8,128)(2,1)} async-done(((bf16[1024,1024]{1,0:T(8,128)(2,1)}), bf16[128,1024]{1,0:T(8,128)(2,1)}) %reduce-scatter.29.cloned.1.call-update) | async-done | bytes 262160 | tf_op jit(solution)/shard_map/reduce_scatter | solution.py:241
  788.2 34.8 %reduce-scatter.33.cloned.1.call-done = bf16[128,2]{1,0:T(8,128)(2,1)} async-done(((bf16[1024,2]{1,0:T(8,128)(2,1)}), bf16[128,2]{1,0:T(8,128)(2,1)}) %reduce-scatter.33.cloned.1.call-update) | async-done | bytes 528
  824.4 35.9 %reduce-scatter.35.cloned.1.call-done = bf16[128,4]{1,0:T(8,128)(2,1)} async-done(((bf16[1024,4]{1,0:T(8,128)(2,1)}), bf16[128,4]{1,0:T(8,128)(2,1)}) %reduce-scatter.35.cloned.1.call-update) | async-done | bytes 1040
  861.6 35.7 %reduce-scatter.25.cloned.1.call-done = bf16[128,256]{1,0:T(8,128)(2,1)} async-done(((bf16[1024,256]{1,0:T(8,128)(2,1)}), bf16[128,256]{1,0:T(8,128)(2,1)}) %reduce-scatter.25.cloned.1.call-update) | async-done | bytes 65552 | tf_op jit(solution)/shard_map/reduce_scatter | solution.py:235
  899.2 14.3 %all-reduce = (f32[512]{0:T(512)}, f32[1024]{0:T(1024)}) all-reduce(f32[512]{0:T(512)S(1)} %add.409, f32[1024]{0:T(1024)S(1)} %add.412), channel_id=1, replica_groups=mesh['fsdp'=4,'ctx'=2,'tp'=4] {'fsdp','ctx'}, use_global_device_ids=true, to_apply=%region_37.38 | all-reduce | flops 1536 | bytes 12288 | tf_op jit(solution)/shard_map/psum | solution.py:251
  913.5 13.4 %reduce-scatter.23.cloned.1.call-done = bf16[2,64,1024]{2,1,0:T(8,128)(2,1)} async-done(((bf16[2,256,1024]{2,1,0:T(8,128)(2,1)}), bf16[2,64,1024]{2,1,0:T(8,128)(2,1)}) %reduce-scatter.23.cloned.1.call-update) | async-done | bytes 262160 | tf_op jit(solution)/shard_map/reduce_scatter | solution.py:217
  928.1 26.8 %reduce-scatter.19.cloned.1.call-done = bf16[2,64,1024]{2,1,0:T(8,128)(2,1)} async-done(((bf16[2,256,1024]{2,1,0:T(8,128)(2,1)}), bf16[2,64,1024]{2,1,0:T(8,128)(2,1)}) %reduce-scatter.19.cloned.1.call-update) | async-done | bytes 262160 | tf_op jit(solution)/shard_map/reduce_scatter | solution.py:217
  957.1 37.7 %reduce-scatter.31.cloned.1.call-done = bf16[128,768]{1,0:T(8,128)(2,1)} async-done(((bf16[1024,768]{1,0:T(8,128)(2,1)}), bf16[128,768]{1,0:T(8,128)(2,1)}) %reduce-scatter.31.cloned.1.call-update) | async-done | bytes 196624
  (272 shorter events, 83.7 us)
Async XLA Ops:
  8.0 75.6 %all-gather.5.cloned.1.call-start = ((), (), s32[]{:S(2)}) async-start(), calls=%async_computation.10 | async-start | bytes 1572864 | tf_op jit(solution)/shard_map/all_gather | solution.py:128
  8.1 8.6 collective-permute-start
  11.1 9.8 collective-permute-start.1
  11.6 3.3 copy-start.40
  13.3 29.1 %copy-start.20 = (bf16[1,2,256,1024]{3,2,1,0:T(8,128)(2,1)}, bf16[1,2,256,1024]{3,2,1,0:T(8,128)(2,1)S(1)}, u32[]{:S(2)}) copy-start(bf16[1,2,256,1024]{3,2,1,0:T(8,128)(2,1)S(1)} %get-tuple-element.113) | copy-start | bytes 3145732
  13.3 36.3 %copy-start.18 = (bf16[1,2,256,1024]{3,2,1,0:T(8,128)(2,1)}, bf16[1,2,256,1024]{3,2,1,0:T(8,128)(2,1)S(1)}, u32[]{:S(2)}) copy-start(bf16[1,2,256,1024]{3,2,1,0:T(8,128)(2,1)S(1)} %get-tuple-element.112) | copy-start | bytes 3145732
  16.7 8.3 collective-permute-start.2
  20.9 8.3 collective-permute-start.3
  25.0 8.4 collective-permute-start.4
  29.2 8.4 collective-permute-start.5
  33.4 8.3 collective-permute-start.6
  55.8 51.2 %copy-start.23 = (f32[2,256,4,1,64]{1,0,4,3,2:T(2,128)}, f32[2,256,4,1,64]{1,0,4,3,2:T(2,128)S(1)}, u32[]{:S(2)}) copy-start(f32[2,256,4,1,64]{1,0,4,3,2:T(2,128)S(1)} %get-tuple-element.114) | copy-start | bytes 1572868
  55.9 2.4 copy-start.42
  55.9 2.5 copy-start.41
  58.2 48.8 %all-gather.11.cloned.1.call-start = ((), (), s32[]{:S(2)}) async-start(), calls=%async_computation.13 | async-start | bytes 1572864 | tf_op jit(solution)/shard_map/all_gather | solution.py:128
  58.3 21.4 %copy-start.39 = (bf16[2,256,4,64]{1,3,2,0:T(8,128)(2,1)S(1)}, bf16[2,256,4,64]{1,3,2,0:T(8,128)(2,1)}, u32[]{:S(2)}) copy-start(bf16[2,256,4,64]{1,3,2,0:T(8,128)(2,1)} %get-tuple-element.144) | copy-start | bytes 786436
  79.6 4.1 copy-start.38
  80.5 191.4 %all-reduce.12.cloned.1.call-start = ((), (), s32[]{:S(2)}) async-start(), calls=%async_computation.26 | async-start | bytes 8388608 | tf_op jit(solution)/shard_map/psum | solution.py:68
  89.6 23.4 %copy-start.31 = (bf16[32,8,2,256]{3,1,2,0:T(8,128)(2,1)}, bf16[32,8,2,256]{3,1,2,0:T(8,128)(2,1)S(1)}, u32[]{:S(2)}) copy-start(bf16[32,8,2,256]{3,1,2,0:T(8,128)(2,1)S(1)} %copy.134) | copy-start | bytes 786436
  113.0 3.6 copy-start.33
  116.7 13.5 %copy-start.43 = (bf16[1024]{0:T(1024)(128)(2,1)S(1)}, bf16[1024]{0:T(1024)(128)(2,1)}, u32[]{:S(2)}) copy-start(bf16[1024]{0:T(1024)(128)(2,1)} %param.18) | copy-start | bytes 6148
  116.7 13.6 %copy-start.46 = (bf16[128,2]{0,1:T(2,128)(2,1)S(1)}, bf16[128,2]{0,1:T(2,128)(2,1)}, u32[]{:S(2)}) copy-start(bf16[128,2]{0,1:T(2,128)(2,1)} %param.20) | copy-start | bytes 1540
  116.7 160.0 %all-gather.7.cloned.1.call-start = ((), (), s32[]{:S(2)}) async-start(), calls=%async_computation.11 | async-start | bytes 2359296 | tf_op jit(solution)/shard_map/all_gather | solution.py:112
  117.3 176.3 %all-gather.9.cloned.1.call-start = ((), (), s32[]{:S(2)}) async-start(), calls=%async_computation.12 | async-start | bytes 2359296 | tf_op jit(solution)/shard_map/all_gather | solution.py:113
  117.9 337.1 %all-reduce.10.cloned.1.call-start = ((), (), s32[]{:S(2)}) async-start(), calls=%async_computation.25 | async-start | bytes 8388608 | tf_op jit(solution)/shard_map/psum | solution.py:68
  275.4 5.0 copy-start.5
  276.7 5.1 copy-start.47
  293.5 4.7 copy-start.36
  293.5 4.7 copy-start.49
  300.8 330.8 %all-reduce.8.cloned.1.call-start = ((), (), s32[]{:S(2)}) async-start(), calls=%async_computation.24 | async-start | bytes 8388608 | tf_op jit(solution)/shard_map/psum | solution.py:68
  459.1 4.2 copy-start.4
  459.2 2.3 copy-start.15
  463.3 2.2 copy-start.57
  463.3 3.2 copy-start.58
  465.0 3.5 copy-start.10
  465.0 6.1 copy-start.13
  466.5 2.0 copy-start.48
  468.5 2.6 copy-start.53
  468.5 2.6 copy-start.54
  468.5 3.3 copy-start.55
  477.5 214.4 %reduce-scatter.21.cloned.1.call-start = ((), (), s32[]{:S(2)}) async-start(), calls=%async_computation.16 | async-start | bytes 1572864 | tf_op jit(solution)/shard_map/reduce_scatter | solution.py:199
  631.7 4.1 copy-start.6
  631.7 4.1 copy-start.9
  631.7 4.7 copy-start.11
  631.7 5.3 copy-start.34
  645.4 3.5 copy-start.3
  651.4 2.3 copy-start.24
  655.3 45.0 %reduce-scatter.17.cloned.1.call-start = ((), (), s32[]{:S(2)}) async-start(), calls=%async_computation.14 | async-start | bytes 1572864 | tf_op jit(solution)/shard_map/reduce_scatter | solution.py:199
  659.7 4.1 copy-start.1
  667.3 3.7 copy-start.52
  667.3 74.7 %reduce-scatter.27.cloned.1.call-start = ((), (), s32[]{:S(2)}) async-start(), calls=%async_computation.19 | async-start | bytes 2359296 | tf_op jit(solution)/shard_map/reduce_scatter | solution.py:238
  667.5 3.5 copy-start.7
  673.9 3.5 copy-start.37
  673.9 112.4 %reduce-scatter.29.cloned.1.call-start = ((), (), s32[]{:S(2)}) async-start(), calls=%async_computation.20 | async-start | bytes 2359296 | tf_op jit(solution)/shard_map/reduce_scatter | solution.py:241
  674.0 3.4 copy-start.14
  680.3 2.9 copy-start.32
  680.3 142.6 %reduce-scatter.33.cloned.1.call-start = ((), (), s32[]{:S(2)}) async-start(), calls=%async_computation.22 | async-start | bytes 294912
  685.2 175.0 %reduce-scatter.35.cloned.1.call-start = ((), (), s32[]{:S(2)}) async-start(), calls=%async_computation.23 | async-start | bytes 294912
  686.3 211.1 %reduce-scatter.25.cloned.1.call-start = ((), (), s32[]{:S(2)}) async-start(), calls=%async_computation.18 | async-start | bytes 589824 | tf_op jit(solution)/shard_map/reduce_scatter | solution.py:235
  689.2 237.7 %reduce-scatter.23.cloned.1.call-start = ((), (), s32[]{:S(2)}) async-start(), calls=%async_computation.17 | async-start | bytes 1310720 | tf_op jit(solution)/shard_map/reduce_scatter | solution.py:217
  697.6 257.3 %reduce-scatter.19.cloned.1.call-start = ((), (), s32[]{:S(2)}) async-start(), calls=%async_computation.15 | async-start | bytes 1310720 | tf_op jit(solution)/shard_map/reduce_scatter | solution.py:217
  706.9 288.0 %reduce-scatter.31.cloned.1.call-start = ((), (), s32[]{:S(2)}) async-start(), calls=%async_computation.21 | async-start | bytes 1769472
  718.8 180.0 %copy-start.28 = (f32[2,256,4,128]{1,3,2,0:T(8,128)S(1)}, f32[2,256,4,128]{1,3,2,0:T(8,128)}, u32[]{:S(2)}) copy-start(f32[2,256,4,128]{1,3,2,0:T(8,128)} %copy-done.27) | copy-start | bytes 3145732
  718.8 180.1 %copy-start.26 = (f32[2,256,4,128]{1,3,2,0:T(8,128)S(1)}, f32[2,256,4,128]{1,3,2,0:T(8,128)}, u32[]{:S(2)}) copy-start(f32[2,256,4,128]{1,3,2,0:T(8,128)} %copy-done.25) | copy-start | bytes 3145732
  (19 other events, 26.9 us)
Sparse Core Ops, SparseCore 0:
  58.3 25.2 all-gather.4
  85.8 21.2 all-gather.10
  116.8 155.0 all-reduce.11
  301.0 153.9 all-reduce.9
  477.7 153.9 all-reduce.7
  655.4 19.3 reduce-scatter.20
  677.1 20.3 reduce-scatter.16
  700.8 41.1 reduce-scatter.26
  745.2 41.1 reduce-scatter.28
  789.2 33.6 reduce-scatter.32
  826.5 33.6 reduce-scatter.34
  863.1 34.1 reduce-scatter.24
  899.6 27.2 reduce-scatter.22
  929.1 25.7 reduce-scatter.18
  958.0 36.7 reduce-scatter.30
Sparse Core Ops, SparseCore 1:
  119.1 27.6 all-gather.6
  148.5 27.6 all-gather.8
